TPU v7x, 256 devices: a whole 4x4x8 slice. The times are simulated.
256 devices in a mesh: member: 8 (over x, z_hi), rows: 32 (over y, z_lo, core).
Axes of the slice: x: 4, y: 4, z: 8 (z_hi: 2, z_lo: 4; z = z_hi * 4 + z_lo), core: 2. Of those that a mesh axis runs over, the one named last changes fastest.
Arguments:
- member_latent_state: bfloat16 [16, 128, 64, 512], P('member', 'rows'), as said below
- analysis_target_field: bfloat16 [128, 64, 512], P('rows'), may hold values from -8 to 8
- conv_first: bfloat16 [512, 9, 512], replicated, may hold values from -0.09375 to 0.09375
- second_kernel_weight: bfloat16 [512, 9, 512], replicated, may hold values from -0.09375 to 0.09375
Outputs:
- ensemble_prognosis_field: bfloat16 [16, 128, 64, 512], P('member', 'rows')
- initial_conv_derivative: float32 [512, 9, 512], P('rows')
- final_filter_slope: float32 [512, 9, 512], P('rows')
Inputs may be any that keep to these rules, and one draw needn't show every extreme that they name: `member_latent_state`: each member's field is drawn independently.
All inputs are finite; a program needn't handle non-finite values.
Results may differ from a plain program's by a relative error of at most 0.0058.
Values may be sent and summed in bfloat16 or wider, within the bound.
A program may use at most 192 MiB of HBM per device.

v0:
```python
import jax
import jax.numpy as jnp
from jax import lax
from jax.sharding import PartitionSpec as P

SOFTENING_EPS = 0.1
INV_ROOT_TWO = 0.7071067811865476
INV_ROOT_TWOPI = 0.3989422804014327


def padded_2(block, sides, width):
    for axis, dim in sides:
        count = lax.axis_size(axis)
        forward = [(i, i + 1) for i in range(count - 1)]
        backward = [(target, source) for source, target in forward]
        low = lax.ppermute(
            lax.slice_in_dim(block, block.shape[dim] - width, None, axis=dim), axis, forward
        )
        high = lax.ppermute(lax.slice_in_dim(block, 0, width, axis=dim), axis, backward)
        block = jnp.concatenate([low, block, high], axis=dim)
    return block


def gelu_value(pre):
    return 0.5 * pre * (1.0 + lax.erf(pre * INV_ROOT_TWO))


def gelu_slope(pre):
    return (
        0.5 * (1.0 + lax.erf(pre * INV_ROOT_TWO)) + pre * jnp.exp(-0.5 * pre * pre) * INV_ROOT_TWOPI
    )


def pad_columns(field):
    return jnp.pad(field, ((0, 0), (0, 0), (1, 1), (0, 0)))


def slab_padded(field):
    extended = padded_2(field, (("rows", 1),), 1)
    return pad_columns(extended)


def haloed_adjoint(field):
    extended = padded_2(field, (("rows", 1),), 1)
    return pad_columns(extended)


def tap_view(padded, tap_index, meridian_extent, longitude_length):
    down = tap_index // 3
    across = tap_index % 3
    return padded[:, down : down + meridian_extent, across : across + longitude_length, :]


def apply_kernel_stencil(padded, kernel, meridian_extent, longitude_length):
    channels = padded.shape[3]
    summed = jnp.zeros(
        (padded.shape[0] * meridian_extent * longitude_length, kernel.shape[2]), jnp.float32
    )
    for tap_index in range(9):
        view = tap_view(padded, tap_index, meridian_extent, longitude_length).reshape(-1, channels)
        summed = summed + jnp.dot(view, kernel[:, tap_index, :], preferred_element_type=jnp.float32)
    return summed.reshape(padded.shape[0], meridian_extent, longitude_length, kernel.shape[2])


def reversed_stencil(padded, kernel, meridian_extent, longitude_length):
    channels = padded.shape[3]
    summed = jnp.zeros(
        (padded.shape[0] * meridian_extent * longitude_length, kernel.shape[0]), jnp.float32
    )
    for tap_index in range(9):
        view = tap_view(padded, 8 - tap_index, meridian_extent, longitude_length).reshape(
            -1, channels
        )
        summed = summed + lax.dot_general(
            view,
            kernel[:, tap_index, :],
            (((1,), (1,)), ((), ())),
            preferred_element_type=jnp.float32,
        )
    return summed.reshape(padded.shape[0], meridian_extent, longitude_length, kernel.shape[0])


def tap_terms(padded, flat_cot, meridian_extent, longitude_length):
    channels = padded.shape[3]
    taps_list = []
    for tap_index in range(9):
        view = tap_view(padded, tap_index, meridian_extent, longitude_length).reshape(-1, channels)
        taps_list.append(
            lax.dot_general(
                view, flat_cot, (((0,), (0,)), ((), ())), preferred_element_type=jnp.float32
            )
        )
    return jnp.stack(taps_list, axis=1)


def stencil_derivative(padded, cotangent, meridian_extent, longitude_length):
    flat_cot = cotangent.reshape(-1, cotangent.shape[3])
    own_share = lax.psum_scatter(
        tap_terms(padded, flat_cot, meridian_extent, longitude_length),
        "rows",
        scatter_dimension=0,
        tiled=True,
    )
    return lax.psum(own_share, "member")


def attraction_sum(local, everyone):

    def step(running, other):
        spread = local - other[None]
        smooth_abs = jnp.sqrt(spread * spread + SOFTENING_EPS * SOFTENING_EPS)
        return (running + spread / smooth_abs, None)

    result, unused = lax.scan(step, jnp.zeros(local.shape, jnp.float32), everyone)
    return result


def predicted_gradient(
    model_output_field,
    measured_truth_field,
    pairwise_spread_part,
    ensemble_draw_count,
    row_sum_complete,
):
    prognosis_misfit = model_output_field - measured_truth_field
    distance_to_analysis = jnp.sqrt(
        prognosis_misfit * prognosis_misfit + SOFTENING_EPS * SOFTENING_EPS
    )
    return (
        prognosis_misfit / distance_to_analysis / ensemble_draw_count
        - pairwise_spread_part / (ensemble_draw_count * (ensemble_draw_count - 1.0))
    ) / row_sum_complete


def body(member_latent_state, analysis_target_field, conv_first, second_kernel_weight):
    meridian_extent = member_latent_state.shape[1]
    longitude_length = member_latent_state.shape[2]
    ensemble_draw_count = float(member_latent_state.shape[0] * lax.axis_size("member"))
    row_sum_complete = float(meridian_extent * lax.axis_size("rows"))
    padded_state = slab_padded(member_latent_state)
    pre_first = apply_kernel_stencil(padded_state, conv_first, meridian_extent, longitude_length)
    hidden = gelu_value(pre_first).astype(jnp.bfloat16)
    hidden_state_bordered = slab_padded(hidden)
    model_output_field = member_latent_state.astype(jnp.float32) + apply_kernel_stencil(
        hidden_state_bordered, second_kernel_weight, meridian_extent, longitude_length
    )
    ensemble_prognosis_field = model_output_field.astype(jnp.bfloat16)
    pairwise_spread_part = attraction_sum(
        model_output_field, lax.all_gather(model_output_field, "member", axis=0, tiled=True)
    )
    measured_truth_field = analysis_target_field.astype(jnp.float32)[None]
    activation_gradient_factor = predicted_gradient(
        model_output_field,
        measured_truth_field,
        pairwise_spread_part,
        ensemble_draw_count,
        row_sum_complete,
    )
    output_cotangent_field = activation_gradient_factor.astype(jnp.bfloat16)
    final_filter_slope = stencil_derivative(
        hidden_state_bordered, output_cotangent_field, meridian_extent, longitude_length
    )
    intermediate_adjoint = reversed_stencil(
        haloed_adjoint(output_cotangent_field),
        second_kernel_weight,
        meridian_extent,
        longitude_length,
    )
    cot_pre = (intermediate_adjoint * gelu_slope(pre_first)).astype(jnp.bfloat16)
    initial_conv_derivative = stencil_derivative(
        padded_state, cot_pre, meridian_extent, longitude_length
    )
    return (ensemble_prognosis_field, initial_conv_derivative, final_filter_slope)


def solution(mesh):
    in_specs = (P("member", "rows", None, None), P("rows", None, None), P(), P())
    out_specs = (P("member", "rows", None, None), P("rows", None, None), P("rows", None, None))
    return jax.shard_map(body, mesh=mesh, in_specs=in_specs, out_specs=out_specs, check_vma=False)
```

profile of v0, /device:TPU:8, one launch (start us, length us, event | category | flops | bytes accessed | tf_op | source)
XLA Modules:
  0.0 734.1 jit_solution(73099665500884084)
XLA Ops:
  8.4 2.1 collective-permute-start
  10.4 6.3 collective-permute-start.1
  25.5 2.2 collective-permute-start.2
  27.7 6.6 collective-permute-start.3
  35.0 1.8 collective-permute-done.3
  43.1 1.8 convert_element_type.29
  44.9 175.7 %all-gather.2.cloned.1.call-done = f32[16,4,64,512]{3,2,1,0:T(8,128)} async-done(((f32[2,4,64,512]{3,2,1,0:T(8,128)}), f32[16,4,64,512]{3,2,1,0:T(8,128)}) %all-gather.2.cloned.1.call-update) | async-done | bytes 8388624 | tf_op jit(solution)/shard_map/all_gather | solution.py:149
  220.6 47.6 %while.11 = (s32[]{:T(128)}, f32[2,4,64,512]{3,2,1,0:T(8,128)S(1)}, f32[16,4,64,512]{3,2,1,0:T(8,128)}, f32[2,4,64,512]{3,2,1,0:T(8,128)}, s32[]{:T(128)}, /*index=5*/s32[]{:T(128)}) while((s32[]{:T(128)}, f32[2,4,64,512]{3,2,1,0:T(8,128)S(1)}, f32[16,4,64,512]{3,2,1,0:T(8,128)}, f32[2,4,64,512]{3,2,1,0:T(8,128)}, s32[]{:T(128)}, ...), condition=%wide.region_1.2_spmd.clone, body=%wide.region_0.1_spmd.clone.sunk | while | flops 1572867 | bytes 4718683 | solution.py:114
  221.7 1.9 select_add_fusion.2
  224.6 1.9 select_add_fusion.2
  227.6 1.9 select_add_fusion.2
  230.6 1.9 select_add_fusion.2
  233.6 1.9 select_add_fusion.2
  236.5 1.9 select_add_fusion.2
  239.5 1.9 select_add_fusion.2
  242.5 1.9 select_add_fusion.2
  245.5 1.9 select_add_fusion.2
  248.5 1.9 select_add_fusion.2
  251.4 1.9 select_add_fusion.2
  254.4 1.9 select_add_fusion.2
  257.4 1.9 select_add_fusion.2
  260.4 1.9 select_add_fusion.2
  263.3 1.9 select_add_fusion.2
  266.3 1.9 select_add_fusion.2
  268.2 1.8 multiply_convert_fusion
  270.0 1.4 fusion.11
  272.9 1.5 fusion.10
  274.4 1.4 fusion.9
  277.2 1.5 fusion.7
  278.7 1.5 fusion.6
  280.2 1.5 fusion.1
  281.7 1.5 fusion.5
  284.2 1.9 collective-permute-start.4
  286.1 6.5 collective-permute-start.5
  293.5 1.6 collective-permute-done.5
  295.9 1.9 fusion.57
  302.1 1.5 fusion.18
  303.6 1.4 fusion.4
  305.1 1.4 fusion.17
  306.5 1.4 fusion.16
  307.9 1.5 fusion.15
  309.4 1.4 fusion.14
  312.3 1.5 fusion.3
  315.3 108.2 %reduce-scatter.5.cloned.1.call-done = f32[16,9,512]{2,0,1:T(8,128)} async-done(((f32[512,9,512]{2,0,1:T(8,128)}), f32[16,9,512]{2,0,1:T(8,128)}) %reduce-scatter.5.cloned.1.call-update) | async-done | bytes 294928 | tf_op jit(solution)/shard_map/reduce_scatter | solution.py:98
  423.5 164.0 %reduce-scatter.3.cloned.1.call-done = f32[16,9,512]{2,0,1:T(8,128)} async-done(((f32[512,9,512]{2,0,1:T(8,128)}), f32[16,9,512]{2,0,1:T(8,128)}) %reduce-scatter.3.cloned.1.call-update) | async-done | bytes 294928 | tf_op jit(solution)/shard_map/reduce_scatter | solution.py:98
  587.5 136.6 %all-reduce.6.cloned.1.call-done = (f32[16,9,512]{2,0,1:T(8,128)}, f32[16,9,512]{2,0,1:T(8,128)}) async-done(((f32[16,9,512]{2,0,1:T(8,128)}, f32[16,9,512]{2,0,1:T(8,128)}), (f32[16,9,512]{2,0,1:T(8,128)}, f32[16,9,512]{2,0,1:T(8,128)})) %all-reduce.6.cloned.1.call-update) | async-done | bytes 589840 | tf_op jit(solution)/shard_map/psum | solution.py:104
  724.2 1.7 copy.54
  725.9 1.7 copy.55
  (119 shorter events, 46.5 us)
Async XLA Ops:
  7.2 13.0 %copy-start.2 = (bf16[2,4,64,512]{3,2,1,0:T(8,128)(2,1)S(1)}, bf16[2,4,64,512]{3,2,1,0:T(8,128)(2,1)}, u32[]{:S(2)}) copy-start(bf16[2,4,64,512]{3,2,1,0:T(8,128)(2,1)} %param.6) | copy-start | bytes 1572868
  7.2 213.4 %all-gather.2.cloned.1.call-start = ((), (), s32[]{:S(2)}) async-start(), calls=%async_computation.2 | async-start | bytes 9437184 | tf_op jit(solution)/shard_map/all_gather | solution.py:149
  7.2 13.7 %slice-start.4 = ((s8[4718592]{0:T(1024)(128)(4,1)}), s8[4194304]{0:T(1024)(128)(4,1)S(1)}, s32[]{:S(2)}) async-start(s8[4718592]{0:T(1024)(128)(4,1)} %bitcast.305), calls=%async_computation.10 | async-start | bytes 8388608
  8.4 9.1 %collective-permute-start = (bf16[2,1,64,512]{3,2,1,0:T(8,128)(2,1)S(1)}, bf16[2,1,64,512]{3,2,1,0:T(8,128)(2,1)S(1)}, u32[]{:S(2)}, u32[]{:S(2)}) collective-permute-start(bf16[2,1,64,512]{3,2,1,0:T(8,128)(2,1)S(1)} %get-tuple-element.81), channel_id=1, source_target_pairs={{0,1},{1,2},{2,3},{3,4},{4,5},{5,6},{6,7},{7,8},{8,9},{9,10},{10,1... | collective-permute-start | bytes 393224 | tf_op jit(solution)/shard_map/ppermute | solution.py:16
  10.4 8.8 %collective-permute-start.1 = (bf16[2,1,64,512]{3,2,1,0:T(8,128)(2,1)S(1)}, bf16[2,1,64,512]{3,2,1,0:T(8,128)(2,1)S(1)}, u32[]{:S(2)}, u32[]{:S(2)}) collective-permute-start(bf16[2,1,64,512]{3,2,1,0:T(8,128)(2,1)S(1)} %get-tuple-element.82), channel_id=1, source_target_pairs={{1,0},{2,1},{3,2},{4,3},{5,4},{6,5},{7,6},{8,7},{9,8},{10,9},{11,1... | collective-permute-start | bytes 393224 | tf_op jit(solution)/shard_map/ppermute | solution.py:19
  18.7 1.5 copy-start.9
  19.3 0.8 copy-start.7
  20.2 1.0 slice-start.5
  24.8 12.7 %slice-start = ((s8[4718592]{0:T(1024)(128)(4,1)}), s8[4194304]{0:T(1024)(128)(4,1)S(1)}, s32[]{:S(2)}) async-start(s8[4718592]{0:T(1024)(128)(4,1)} %bitcast.297), calls=%async_computation.6 | async-start | bytes 8388608
  25.2 14.2 %copy-start = (f32[512,512]{1,0:T(8,128)}, f32[512,512]{1,0:T(8,128)S(1)}, u32[]{:S(2)}) copy-start(f32[512,512]{1,0:T(8,128)S(1)} %fusion.21) | copy-start | bytes 3145732
  25.5 12.5 %copy-start.5 = (bf16[2,4,64,512]{3,2,1,0:T(8,128)(2,1)}, bf16[2,4,64,512]{3,2,1,0:T(8,128)(2,1)S(1)}, u32[]{:S(2)}) copy-start(bf16[2,4,64,512]{3,2,1,0:T(8,128)(2,1)S(1)} %multiply_convert_fusion.2) | copy-start | bytes 1572868
  25.5 9.5 %collective-permute-start.2 = (bf16[2,1,64,512]{3,2,1,0:T(8,128)(2,1)S(1)}, bf16[2,1,64,512]{3,2,1,0:T(8,128)(2,1)S(1)}, u32[]{:S(2)}, u32[]{:S(2)}) collective-permute-start(bf16[2,1,64,512]{3,2,1,0:T(8,128)(2,1)S(1)} %get-tuple-element.77), channel_id=1, source_target_pairs={{0,1},{1,2},{2,3},{3,4},{4,5},{5,6},{6,7},{7,8},{8,9},{9,10},{10,1... | collective-permute-start | bytes 393224 | tf_op jit(solution)/shard_map/ppermute | solution.py:16
  27.7 9.8 %slice-start.1 = ((s8[4718592]{0:T(1024)(128)(4,1)}), s8[524288]{0:T(1024)(128)(4,1)S(1)}, s32[]{:S(2)}) async-start(s8[4718592]{0:T(1024)(128)(4,1)} %bitcast.297), calls=%async_computation.7 | async-start | bytes 1048576
  27.7 9.1 %collective-permute-start.3 = (bf16[2,1,64,512]{3,2,1,0:T(8,128)(2,1)S(1)}, bf16[2,1,64,512]{3,2,1,0:T(8,128)(2,1)S(1)}, u32[]{:S(2)}, u32[]{:S(2)}) collective-permute-start(bf16[2,1,64,512]{3,2,1,0:T(8,128)(2,1)S(1)} %get-tuple-element.78), channel_id=1, source_target_pairs={{1,0},{2,1},{3,2},{4,3},{5,4},{6,5},{7,6},{8,7},{9,8},{10,9},{11,1... | collective-permute-start | bytes 393224 | tf_op jit(solution)/shard_map/ppermute | solution.py:19
  35.0 3.0 copy-start.11
  43.0 380.4 %reduce-scatter.5.cloned.1.call-start = ((), (), s32[]{:S(2)}) async-start(), calls=%async_computation.4 | async-start | bytes 9732096 | tf_op jit(solution)/shard_map/reduce_scatter | solution.py:98
  268.2 3.2 copy-start.6
  268.2 3.2 copy-start.12
  270.0 11.6 %copy-start.3 = (bf16[2,4,64,512]{3,2,1,0:T(8,128)(2,1)}, bf16[2,4,64,512]{3,2,1,0:T(8,128)(2,1)S(1)}, u32[]{:S(2)}) copy-start(bf16[2,4,64,512]{3,2,1,0:T(8,128)(2,1)S(1)} %multiply_convert_fusion) | copy-start | bytes 1572868
  283.1 1.0 copy-start.4
  283.1 304.4 %reduce-scatter.3.cloned.1.call-start = ((), (), s32[]{:S(2)}) async-start(), calls=%async_computation.3 | async-start | bytes 9732096 | tf_op jit(solution)/shard_map/reduce_scatter | solution.py:98
  284.2 9.3 %collective-permute-start.4 = (bf16[2,1,64,512]{3,2,1,0:T(8,128)(2,1)S(1)}, bf16[2,1,64,512]{3,2,1,0:T(8,128)(2,1)S(1)}, u32[]{:S(2)}, u32[]{:S(2)}) collective-permute-start(bf16[2,1,64,512]{3,2,1,0:T(8,128)(2,1)S(1)} %get-tuple-element.73), channel_id=1, source_target_pairs={{0,1},{1,2},{2,3},{3,4},{4,5},{5,6},{6,7},{7,8},{8,9},{9,10},{10,1... | collective-permute-start | bytes 393224 | tf_op jit(solution)/shard_map/ppermute | solution.py:16
  286.1 9.0 %collective-permute-start.5 = (bf16[2,1,64,512]{3,2,1,0:T(8,128)(2,1)S(1)}, bf16[2,1,64,512]{3,2,1,0:T(8,128)(2,1)S(1)}, u32[]{:S(2)}, u32[]{:S(2)}) collective-permute-start(bf16[2,1,64,512]{3,2,1,0:T(8,128)(2,1)S(1)} %get-tuple-element.74), channel_id=1, source_target_pairs={{1,0},{2,1},{3,2},{4,3},{5,4},{6,5},{7,6},{8,7},{9,8},{10,9},{11,1... | collective-permute-start | bytes 393224 | tf_op jit(solution)/shard_map/ppermute | solution.py:19
  295.2 2.7 slice-start.2
  295.4 2.4 slice-start.3
  300.2 1.5 copy-start.1
  301.2 2.4 copy-start.10
  307.9 4.4 copy-start.8
  315.3 408.9 %all-reduce.6.cloned.1.call-start = ((), (), s32[]{:S(2)}) async-start(), calls=%async_computation.5 | async-start | bytes 1179648 | tf_op jit(solution)/shard_map/psum | solution.py:104
Sparse Core Ops, SparseCore 0:
  43.2 177.3 all-gather.1
  283.3 140.1 reduce-scatter.4
  426.1 161.3 reduce-scatter.2
  590.0 134.0 all-reduce.5
where the time goes:
time: 736 us; the launch traced here: 734 us
  waiting for transfers between devices  591 us (80%)
  matrix products  39.7 us (5%)
  other arithmetic  36.4 us (5%)
  local copies, waits for them, and re-layouts  26.6 us (4%)
  starting transfers between devices  25.8 us (4%)
  between operations  14.3 us (2%)
    reduce_scatter x2, waiting for transfers between devices, stencil_derivative(): lax.psum_scatter(tap_terms(padded, flat_cot, meridian_extent, longitude_l...  272 us
    all_gather x1, waiting for transfers between devices, body(): lax.all_gather(model_output_field, 'member', axis=0, tiled=True)  176 us
    psum x1, waiting for transfers between devices, stencil_derivative(): return lax.psum(own_share, 'member')  137 us
    add x16, other arithmetic, step(): return (running + spread / smooth_abs, None)  30 us
    dot_general x18, matrix products, tap_terms(): lax.dot_general(view, flat_cot, (((0,), (0,)), ((), ())), preferred_eleme...  26.2 us
    ppermute x3, starting transfers between devices, padded_2(): lax.ppermute(lax.slice_in_dim(block, 0, width, axis=dim), axis, backward)  19.5 us
    sub x16, local copies, waits for them, and re-layouts, step(): spread = local - other[None]  17.3 us
  transfers between devices with their start and end apart: 10, of which 10 were waited for; matrix products, arithmetic and copies ran while one was open for 3% of the time, Pallas kernels for 0%

commit v1 on v0

--- a/solution.py
+++ b/solution.py
@@ -101,7 +101,7 @@
         scatter_dimension=0,
         tiled=True,
     )
-    return lax.psum(own_share, "member")
+    return jnp.sum(lax.all_gather(own_share, "member"), axis=0)
 
 
 def attraction_sum(local, everyone):

time: 736 us -> 775 us (1.053)
  waiting for transfers between devices: 591 us -> 628 us
    all_gather x0 -> x2, waiting for transfers between devices: none -> 174 us  [stencil_derivative(): return jnp.sum(lax.all_gather(own_share, 'member'), axis=0)]
    psum x1 -> x0, waiting for transfers between devices: 137 us -> none  [stencil_derivative(): return lax.psum(own_share, 'member')]
  transfers between devices with their start and end apart: 10 -> 11, of which waited for: 10 -> 11; matrix products, arithmetic and copies ran while one was open for 3% -> 3% of each run, Pallas kernels for 0% -> 0%
where the time goes in v1:
time: 775 us; the launch traced here: 773 us
  waiting for transfers between devices  628 us (81%)
  other arithmetic  41.7 us (5%)
  matrix products  39.8 us (5%)
  starting transfers between devices  25.8 us (3%)
  local copies, waits for them, and re-layouts  23.2 us (3%)
  between operations  14.4 us (2%)
    reduce_scatter x2, waiting for transfers between devices, stencil_derivative(): lax.psum_scatter(tap_terms(padded, flat_cot, meridian_extent, longitude_l...  272 us
    all_gather x1, waiting for transfers between devices, body(): lax.all_gather(model_output_field, 'member', axis=0, tiled=True)  176 us
    all_gather x2, waiting for transfers between devices, stencil_derivative(): return jnp.sum(lax.all_gather(own_share, 'member'), axis=0)  174 us
    add x16, other arithmetic, step(): return (running + spread / smooth_abs, None)  30 us
    dot_general x18, matrix products, tap_terms(): lax.dot_general(view, flat_cot, (((0,), (0,)), ((), ())), preferred_eleme...  26.2 us
    ppermute x3, starting transfers between devices, padded_2(): lax.ppermute(lax.slice_in_dim(block, 0, width, axis=dim), axis, backward)  19.5 us
    sub x16, local copies, waits for them, and re-layouts, step(): spread = local - other[None]  17.3 us
  transfers between devices with their start and end apart: 11, of which 11 were waited for; matrix products, arithmetic and copies ran while one was open for 3% of the time, Pallas kernels for 0%

profile of v1, /device:TPU:8, one launch (start us, length us, event | category | flops | bytes accessed | tf_op | source)
XLA Modules:
  0.0 772.8 jit_solution(10107165161634424168)
XLA Ops:
  8.4 2.1 collective-permute-start
  10.4 6.3 collective-permute-start.1
  25.5 2.2 collective-permute-start.2
  27.7 6.6 collective-permute-start.3
  35.0 1.8 collective-permute-done.3
  43.1 1.8 convert_element_type.29
  44.9 175.7 %all-gather.6.cloned.1.call-done = f32[16,4,64,512]{3,2,1,0:T(8,128)} async-done(((f32[2,4,64,512]{3,2,1,0:T(8,128)}), f32[16,4,64,512]{3,2,1,0:T(8,128)}) %all-gather.6.cloned.1.call-update) | async-done | bytes 8388624 | tf_op jit(solution)/shard_map/all_gather | solution.py:149
  220.6 47.6 %while.11 = (s32[]{:T(128)}, f32[2,4,64,512]{3,2,1,0:T(8,128)S(1)}, f32[16,4,64,512]{3,2,1,0:T(8,128)}, f32[2,4,64,512]{3,2,1,0:T(8,128)}, s32[]{:T(128)}, /*index=5*/s32[]{:T(128)}) while((s32[]{:T(128)}, f32[2,4,64,512]{3,2,1,0:T(8,128)S(1)}, f32[16,4,64,512]{3,2,1,0:T(8,128)}, f32[2,4,64,512]{3,2,1,0:T(8,128)}, s32[]{:T(128)}, ...), condition=%wide.region_1.2_spmd.clone, body=%wide.region_0.1_spmd.clone.sunk | while | flops 1572867 | bytes 4718683 | solution.py:114
  221.6 1.9 select_add_fusion.2
  224.6 1.9 select_add_fusion.2
  227.6 1.9 select_add_fusion.2
  230.6 1.9 select_add_fusion.2
  233.6 1.9 select_add_fusion.2
  236.5 1.9 select_add_fusion.2
  239.5 1.9 select_add_fusion.2
  242.5 1.9 select_add_fusion.2
  245.5 1.9 select_add_fusion.2
  248.4 1.9 select_add_fusion.2
  251.4 1.9 select_add_fusion.2
  254.4 1.9 select_add_fusion.2
  257.4 1.9 select_add_fusion.2
  260.4 1.9 select_add_fusion.2
  263.3 1.9 select_add_fusion.2
  266.3 1.9 select_add_fusion.2
  268.2 1.8 multiply_convert_fusion
  270.0 1.4 fusion.11
  272.9 1.5 fusion.10
  274.4 1.4 fusion.9
  277.2 1.5 fusion.7
  278.7 1.4 fusion.6
  280.2 1.5 fusion.1
  281.6 1.5 fusion.5
  284.2 1.9 collective-permute-start.4
  286.1 6.5 collective-permute-start.5
  293.4 1.7 collective-permute-done.5
  295.9 1.9 fusion.57
  302.2 1.5 fusion.18
  305.1 1.5 fusion.17
  308.0 1.5 fusion.15
  309.4 1.5 fusion.14
  312.3 1.5 fusion.3
  313.9 1.5 fusion.12
  315.4 108.8 %reduce-scatter.5.cloned.1.call-done = f32[16,9,512]{2,0,1:T(8,128)} async-done(((f32[512,9,512]{2,0,1:T(8,128)}), f32[16,9,512]{2,0,1:T(8,128)}) %reduce-scatter.5.cloned.1.call-update) | async-done | bytes 294928 | tf_op jit(solution)/shard_map/reduce_scatter | solution.py:98
  424.3 162.8 %reduce-scatter.3.cloned.1.call-done = f32[16,9,512]{2,0,1:T(8,128)} async-done(((f32[512,9,512]{2,0,1:T(8,128)}), f32[16,9,512]{2,0,1:T(8,128)}) %reduce-scatter.3.cloned.1.call-update) | async-done | bytes 294928 | tf_op jit(solution)/shard_map/reduce_scatter | solution.py:98
  587.1 98.5 %all-gather.10.cloned.1.call-done = f32[128,9,512]{2,0,1:T(8,128)} async-done(((f32[16,9,512]{2,0,1:T(8,128)}), f32[128,9,512]{2,0,1:T(8,128)}) %all-gather.10.cloned.1.call-update) | async-done | bytes 2359312 | tf_op jit(solution)/shard_map/all_gather | solution.py:104
  685.6 2.6 reduce_sum.19
  688.3 75.3 %all-gather.8.cloned.1.call-done = f32[128,9,512]{2,0,1:T(8,128)} async-done(((f32[16,9,512]{2,0,1:T(8,128)}), f32[128,9,512]{2,0,1:T(8,128)}) %all-gather.8.cloned.1.call-update) | async-done | bytes 2359312 | tf_op jit(solution)/shard_map/all_gather | solution.py:104
  763.6 2.6 reduce_sum.18
  (122 shorter events, 48.0 us)
Async XLA Ops:
  7.2 13.0 %copy-start.2 = (bf16[2,4,64,512]{3,2,1,0:T(8,128)(2,1)S(1)}, bf16[2,4,64,512]{3,2,1,0:T(8,128)(2,1)}, u32[]{:S(2)}) copy-start(bf16[2,4,64,512]{3,2,1,0:T(8,128)(2,1)} %param.6) | copy-start | bytes 1572868
  7.2 213.4 %all-gather.6.cloned.1.call-start = ((), (), s32[]{:S(2)}) async-start(), calls=%async_computation.2 | async-start | bytes 9437184 | tf_op jit(solution)/shard_map/all_gather | solution.py:149
  7.2 13.7 %slice-start.4 = ((s8[4718592]{0:T(1024)(128)(4,1)}), s8[4194304]{0:T(1024)(128)(4,1)S(1)}, s32[]{:S(2)}) async-start(s8[4718592]{0:T(1024)(128)(4,1)} %bitcast.307), calls=%async_computation.11 | async-start | bytes 8388608
  8.4 9.1 %collective-permute-start = (bf16[2,1,64,512]{3,2,1,0:T(8,128)(2,1)S(1)}, bf16[2,1,64,512]{3,2,1,0:T(8,128)(2,1)S(1)}, u32[]{:S(2)}, u32[]{:S(2)}) collective-permute-start(bf16[2,1,64,512]{3,2,1,0:T(8,128)(2,1)S(1)} %get-tuple-element.79), channel_id=1, source_target_pairs={{0,1},{1,2},{2,3},{3,4},{4,5},{5,6},{6,7},{7,8},{8,9},{9,10},{10,1... | collective-permute-start | bytes 393224 | tf_op jit(solution)/shard_map/ppermute | solution.py:16
  10.4 8.8 %collective-permute-start.1 = (bf16[2,1,64,512]{3,2,1,0:T(8,128)(2,1)S(1)}, bf16[2,1,64,512]{3,2,1,0:T(8,128)(2,1)S(1)}, u32[]{:S(2)}, u32[]{:S(2)}) collective-permute-start(bf16[2,1,64,512]{3,2,1,0:T(8,128)(2,1)S(1)} %get-tuple-element.80), channel_id=1, source_target_pairs={{1,0},{2,1},{3,2},{4,3},{5,4},{6,5},{7,6},{8,7},{9,8},{10,9},{11,1... | collective-permute-start | bytes 393224 | tf_op jit(solution)/shard_map/ppermute | solution.py:19
  18.7 2.2 copy-start.9
  19.3 0.8 copy-start.7
  20.2 1.0 slice-start.5
  24.8 12.7 %slice-start = ((s8[4718592]{0:T(1024)(128)(4,1)}), s8[4194304]{0:T(1024)(128)(4,1)S(1)}, s32[]{:S(2)}) async-start(s8[4718592]{0:T(1024)(128)(4,1)} %bitcast.299), calls=%async_computation.7 | async-start | bytes 8388608
  25.2 14.2 %copy-start = (f32[512,512]{1,0:T(8,128)}, f32[512,512]{1,0:T(8,128)S(1)}, u32[]{:S(2)}) copy-start(f32[512,512]{1,0:T(8,128)S(1)} %fusion.21) | copy-start | bytes 3145732
  25.4 12.5 %copy-start.5 = (bf16[2,4,64,512]{3,2,1,0:T(8,128)(2,1)}, bf16[2,4,64,512]{3,2,1,0:T(8,128)(2,1)S(1)}, u32[]{:S(2)}) copy-start(bf16[2,4,64,512]{3,2,1,0:T(8,128)(2,1)S(1)} %multiply_convert_fusion.2) | copy-start | bytes 1572868
  25.5 9.5 %collective-permute-start.2 = (bf16[2,1,64,512]{3,2,1,0:T(8,128)(2,1)S(1)}, bf16[2,1,64,512]{3,2,1,0:T(8,128)(2,1)S(1)}, u32[]{:S(2)}, u32[]{:S(2)}) collective-permute-start(bf16[2,1,64,512]{3,2,1,0:T(8,128)(2,1)S(1)} %get-tuple-element.75), channel_id=1, source_target_pairs={{0,1},{1,2},{2,3},{3,4},{4,5},{5,6},{6,7},{7,8},{8,9},{9,10},{10,1... | collective-permute-start | bytes 393224 | tf_op jit(solution)/shard_map/ppermute | solution.py:16
  27.7 9.8 %slice-start.1 = ((s8[4718592]{0:T(1024)(128)(4,1)}), s8[524288]{0:T(1024)(128)(4,1)S(1)}, s32[]{:S(2)}) async-start(s8[4718592]{0:T(1024)(128)(4,1)} %bitcast.299), calls=%async_computation.8 | async-start | bytes 1048576
  27.7 9.1 %collective-permute-start.3 = (bf16[2,1,64,512]{3,2,1,0:T(8,128)(2,1)S(1)}, bf16[2,1,64,512]{3,2,1,0:T(8,128)(2,1)S(1)}, u32[]{:S(2)}, u32[]{:S(2)}) collective-permute-start(bf16[2,1,64,512]{3,2,1,0:T(8,128)(2,1)S(1)} %get-tuple-element.76), channel_id=1, source_target_pairs={{1,0},{2,1},{3,2},{4,3},{5,4},{6,5},{7,6},{8,7},{9,8},{10,9},{11,1... | collective-permute-start | bytes 393224 | tf_op jit(solution)/shard_map/ppermute | solution.py:19
  35.0 3.0 copy-start.11
  43.0 381.2 %reduce-scatter.5.cloned.1.call-start = ((), (), s32[]{:S(2)}) async-start(), calls=%async_computation.4 | async-start | bytes 9732096 | tf_op jit(solution)/shard_map/reduce_scatter | solution.py:98
  268.2 3.3 copy-start.6
  268.2 3.2 copy-start.12
  270.0 11.7 %copy-start.3 = (bf16[2,4,64,512]{3,2,1,0:T(8,128)(2,1)}, bf16[2,4,64,512]{3,2,1,0:T(8,128)(2,1)S(1)}, u32[]{:S(2)}) copy-start(bf16[2,4,64,512]{3,2,1,0:T(8,128)(2,1)S(1)} %multiply_convert_fusion) | copy-start | bytes 1572868
  283.1 1.0 copy-start.4
  283.1 303.9 %reduce-scatter.3.cloned.1.call-start = ((), (), s32[]{:S(2)}) async-start(), calls=%async_computation.3 | async-start | bytes 9732096 | tf_op jit(solution)/shard_map/reduce_scatter | solution.py:98
  284.2 9.3 %collective-permute-start.4 = (bf16[2,1,64,512]{3,2,1,0:T(8,128)(2,1)S(1)}, bf16[2,1,64,512]{3,2,1,0:T(8,128)(2,1)S(1)}, u32[]{:S(2)}, u32[]{:S(2)}) collective-permute-start(bf16[2,1,64,512]{3,2,1,0:T(8,128)(2,1)S(1)} %get-tuple-element.71), channel_id=1, source_target_pairs={{0,1},{1,2},{2,3},{3,4},{4,5},{5,6},{6,7},{7,8},{8,9},{9,10},{10,1... | collective-permute-start | bytes 393224 | tf_op jit(solution)/shard_map/ppermute | solution.py:16
  286.1 9.0 %collective-permute-start.5 = (bf16[2,1,64,512]{3,2,1,0:T(8,128)(2,1)S(1)}, bf16[2,1,64,512]{3,2,1,0:T(8,128)(2,1)S(1)}, u32[]{:S(2)}, u32[]{:S(2)}) collective-permute-start(bf16[2,1,64,512]{3,2,1,0:T(8,128)(2,1)S(1)} %get-tuple-element.72), channel_id=1, source_target_pairs={{1,0},{2,1},{3,2},{4,3},{5,4},{6,5},{7,6},{8,7},{9,8},{10,9},{11,1... | collective-permute-start | bytes 393224 | tf_op jit(solution)/shard_map/ppermute | solution.py:19
  295.2 2.7 slice-start.2
  295.5 2.4 slice-start.3
  300.3 1.5 copy-start.1
  301.2 2.4 copy-start.10
  308.0 4.4 copy-start.8
  315.3 370.3 %all-gather.10.cloned.1.call-start = ((), (), s32[]{:S(2)}) async-start(), calls=%async_computation.6 | async-start | bytes 2654208 | tf_op jit(solution)/shard_map/all_gather | solution.py:104
  424.2 339.3 %all-gather.8.cloned.1.call-start = ((), (), s32[]{:S(2)}) async-start(), calls=%async_computation.5 | async-start | bytes 2654208 | tf_op jit(solution)/shard_map/all_gather | solution.py:104
Sparse Core Ops, SparseCore 0:
  43.1 177.3 all-gather.5
  283.2 140.9 reduce-scatter.4
  426.8 160.2 reduce-scatter.2
  589.6 96.0 all-gather.9
  688.1 75.4 all-gather.7
